TPU v7x, 256 devices: a whole 4x4x8 slice. The times are simulated.
256 devices in a mesh: row: 16 (over z, core), col: 16 (over x, y).
Axes of the slice: x: 4, y: 4, z: 8, core: 2. Of those that a mesh axis runs over, the one named last changes fastest.
Arguments:
- positions: float32 [3, 98304], P(None, ('row', 'col')), may hold values from -5 to 5
- velocities: float32 [3, 98304], P(None, ('row', 'col')), may hold values from -5 to 5
- accels: float32 [3, 98304], P(None, ('row', 'col')), may hold values from -12 to 12
- jerks: float32 [3, 98304], P(None, ('row', 'col')), may hold values from -6 to 6
- masses: float32 [98304], P(('row', 'col')), may hold values from 0.2 to 5
- star_time: float32 [98304], P(('row', 'col')), may hold values from -0.3 to 0
- block_steps: float32 [1], replicated, may hold values from 0.1 to 0.3
- act_index: int32 [1, 32768], P(None, ('row', 'col')), may hold values from 0 to 383, as said below
- act_count: int32 [1, 256], P(None, ('row', 'col')), may hold values from 1 to 128, 8192 in all within a row
Outputs:
- new_positions: float32 [3, 98304], P(None, ('row', 'col'))
- new_velocities: float32 [3, 98304], P(None, ('row', 'col'))
- new_accels: float32 [3, 98304], P(None, ('row', 'col'))
- new_jerks: float32 [3, 98304], P(None, ('row', 'col'))
Inputs may be any that keep to these rules, and one draw needn't show every extreme that they name: `act_index`: in each block step the 128 entries of one device are distinct local star numbers of that device; only the first act_count entries are active. Each row of act_count is one block step; its entries, one for each device, sum to 32 times the number of devices over all devices together.
All inputs are finite; a program needn't handle non-finite values.
Results may differ from a plain program's by a relative error of at most 0.00017.
Values sent between devices are 32-bit elements; how exact they have to be, the bound alone decides.
A program may use at most 64 MiB of HBM per device.

v0:
```python
import functools
import math

import jax
import jax.numpy as jnp
from jax import lax
from jax.experimental import pallas as pl
from jax.experimental.pallas import tpu as pltpu
from jax.sharding import PartitionSpec as P

SOFTENING = 0.0025
GRAVITY = 8.0
LANES = 128
ROWS = 2
AHEAD = 2
SPAN = 2
GRANT = 8 << 20
MESH = pl.DeviceIdType.MESH
HIGHEST = lax.Precision.HIGHEST


def predict(pos, vel, acc, jerk, elapsed):
    square = elapsed * elapsed
    pred_pos = pos + vel * elapsed + acc * (square * 0.5) + jerk * (square * elapsed / 6.0)
    pred_vel = vel + acc * elapsed + jerk * (square * 0.5)
    return pred_pos, pred_vel


def near(step, size):
    return min(step, size - step)


def plane_peers(n_col):
    side = math.isqrt(n_col)
    row, col = lax.axis_index("row"), lax.axis_index("col")
    x, y, core = lax.div(col, side), lax.rem(col, side), lax.rem(row, ROWS)
    xs = [lax.rem(x + i, side) * side for i in range(side)]
    ys = [lax.rem(y + i, side) for i in range(side)]
    rows = [row - core + lax.rem(core + i, ROWS) for i in range(ROWS)]
    peers = []
    for i in range(ROWS):
        for j in range(side):
            for k in range(side):
                slot = (i * side + j) * side + k
                back = ((-i % ROWS) * side + (-j % side)) * side + (-k % side)
                far = near(j, side) + near(k, side)
                peers.append((far, slot, back, (rows[i], xs[j] + ys[k])))
    return sorted(peers[1:], key=lambda peer: -peer[0])


def line_peers(n_row):
    size = n_row // ROWS
    row, col = lax.axis_index("row"), lax.axis_index("col")
    place, core = lax.div(row, ROWS), lax.rem(row, ROWS)
    peers = [
        (near(i, size), i, size - i, (lax.rem(place + i, size) * ROWS + core, col))
        for i in range(1, size)
    ]
    return sorted(peers, key=lambda peer: -peer[0])


def greet(peers):
    barrier = pltpu.get_barrier_semaphore()
    for _, _, _, device in sorted(peers, key=lambda peer: -peer[0]):
        pl.semaphore_signal(barrier, inc=1, device_id=device, device_id_type=MESH)


def one_hot(index_row, count, stars):
    star = lax.broadcasted_iota(jnp.int32, (stars, LANES), 0)
    slot = lax.broadcasted_iota(jnp.int32, (stars, LANES), 1)
    return jnp.where((star == index_row) & (slot < count), 1.0, 0.0)


def exchange_kernel(
    n_row, n_col, strength,
    step_ref, count_ref, *refs,
):
    inputs, (tgt_ref, src_ref, cnt_ref), rest = refs[:7], refs[7:10], refs[10:]
    local, (load_sem, send_a, recv_a, send_b, recv_b) = rest[:7], rest[7:]
    pos_ref, vel_ref, acc_ref, jerk_ref, mass_ref, time_ref, index_ref = local
    n_a, n_b = ROWS * n_col, n_row // ROWS
    plane, line = plane_peers(n_col), line_peers(n_row)
    loads = [
        pltpu.make_async_copy(a, b, load_sem.at[i]) for i, (a, b) in enumerate(zip(inputs, local))
    ]
    for load in loads:
        load.start()
    greet(plane + line)
    for load in loads:
        load.wait()

    stars = pos_ref.shape[1]
    elapsed = step_ref[0] - time_ref[...].reshape(1, stars)
    pred_pos, pred_vel = predict(pos_ref[...], vel_ref[...], acc_ref[...], jerk_ref[...], elapsed)
    weight = mass_ref[...].reshape(1, stars) * strength
    packet = jnp.concatenate([pred_pos, pred_vel, weight, jnp.zeros_like(weight)], axis=0)
    src_ref[0] = packet
    count = count_ref[0, 0]
    chosen = jnp.dot(
        packet, one_hot(index_ref[...], LANES, stars), precision=HIGHEST,
        preferred_element_type=jnp.float32,
    )
    comp = lax.broadcasted_iota(jnp.int32, (8, LANES), 0)
    tgt_ref[0] = jnp.where(comp == 6, count.astype(jnp.float32), chosen)

    pl.semaphore_wait(pltpu.get_barrier_semaphore(), n_a + n_b - 2)
    far = [
        pltpu.make_async_remote_copy(
            src_ref=src_ref.at[0], dst_ref=src_ref.at[back],
            send_sem=send_b.at[slot], recv_sem=recv_b.at[back],
            device_id=device, device_id_type=MESH,
        )
        for _, slot, back, device in line
    ]
    wide = [
        pltpu.make_async_remote_copy(
            src_ref=tgt_ref.at[0], dst_ref=tgt_ref.at[back],
            send_sem=send_a.at[slot], recv_sem=recv_a.at[back],
            device_id=device, device_id_type=MESH,
        )
        for _, slot, back, device in plane
    ]
    for copy in far + wide:
        copy.start()
    for copy in wide:
        copy.wait()
    lane = lax.broadcasted_iota(jnp.int32, (1, LANES), 1)
    counts = jnp.zeros((1, LANES), jnp.float32)
    for k in range(n_a):
        counts = jnp.where(lane == k, tgt_ref[k, 6:7, :], counts)
    cnt_ref[...] = counts.astype(jnp.int32)
    for copy in far:
        copy.wait()


def split3(x):
    high = x.astype(jnp.bfloat16).astype(jnp.float32)
    rest = x - high
    mid = rest.astype(jnp.bfloat16).astype(jnp.float32)
    return high, mid, (rest - mid).astype(jnp.bfloat16).astype(jnp.float32)


def grid3(x):
    coarse = jnp.floor(x * 8.0 + 0.5) * 0.125
    rest = x - coarse
    fine = jnp.floor(rest * 4096.0 + 0.5) * (1.0 / 4096.0)
    return coarse, fine, (rest - fine).astype(jnp.bfloat16).astype(jnp.float32)


def sum3(x):
    return x[0:1] + x[1:2] + x[2:3]


def levels(state):
    xg, xm, xr = grid3(state[0:3])
    vh, vm, vl = split3(state[3:6])
    x, v = xg + xm + xr, vh + vm + vl
    scalars = [
        sum3(x * v),
        sum3(xg * xg + 2.0 * (xg * xm)),
        sum3(xm * xm + 2.0 * (xg * xr) + 2.0 * (xm * xr) + xr * xr),
    ]
    return (xg, xm, xr), (vh, vm, vl), scalars


def source_features(state):
    xs, vs, (s, ab, c) = levels(state)
    one = jnp.ones_like(state[0:1])
    none = jnp.zeros_like(one)
    s, ab, c = split3(s), split3(ab), split3(c)
    g = jnp.concatenate([xs[0], vs[0], s[0], one], axis=0)
    m = jnp.concatenate([xs[1], vs[1], s[1], none], axis=0)
    r = jnp.concatenate([xs[2], vs[2], s[2], none], axis=0)
    e = jnp.concatenate([*ab, one, none, none, none, none], axis=0)
    f = jnp.concatenate([*c, one, one, none, none, none], axis=0)
    return jnp.concatenate([g, g, m, e, g, m, m, r, r, r, f, jnp.zeros_like(f)], axis=0)


def target_features(state):
    xs, vs, (s, ab, c) = levels(state)
    one = jnp.ones_like(state[0:1])
    none = jnp.zeros_like(one)
    void = jnp.zeros_like(state[0:3])
    zero = jnp.zeros_like(state)
    s, ab, c = split3(s), split3(ab), split3(c + SOFTENING)
    x2 = [-2.0 * z for z in xs]
    xs, vs = [-z for z in xs], [-z for z in vs]

    def block(*rows):
        return jnp.concatenate(rows, axis=0)

    radial = block(
        vs[0], xs[0], one, s[0],
        vs[1], xs[1], none, s[1],
        vs[0], xs[0], one, none,
        zero,
        vs[2], xs[2], none, s[2],
        vs[1], xs[1], none, none,
        zero,
        vs[0], xs[0], one, none,
        zero, zero, zero, zero,
    )
    square = block(
        x2[0], void, none, ab[0],
        x2[1], void, none, ab[1],
        x2[0], void, none, none,
        one, one, one, ab[2], void, none,
        x2[2], void, none, c[0],
        x2[1], void, none, none,
        x2[2], void, none, none,
        x2[0], void, none, none,
        x2[1], void, none, none,
        x2[2], void, none, none,
        one, one, one, c[1], c[2], void,
        zero,
    )
    return jnp.concatenate([radial, square], axis=1).astype(jnp.bfloat16)


def force_kernel(cnt_ref, tgt_ref, src_ref, out_ref, dense, src_t, packed, offs):
    n_a, n_b, stars = tgt_ref.shape[0], src_ref.shape[0], src_ref.shape[2]
    per = stars // LANES
    parts = n_b * per
    f32, bf16 = jnp.float32, jnp.bfloat16
    comp = lax.broadcasted_iota(jnp.int32, (8, LANES), 0)
    lane = lax.broadcasted_iota(jnp.int32, (8, LANES), 1)

    def piece(j):
        b, p = j // per, j % per
        return src_ref[b, :, p * LANES : (p + 1) * LANES]

    top = bottom = piece(0)
    for j in range(1, parts):
        top, bottom = jnp.maximum(top, piece(j)), jnp.minimum(bottom, piece(j))
    middle = jnp.max(top, axis=1, keepdims=True) + jnp.min(bottom, axis=1, keepdims=True)
    middle = jnp.where(comp < 6, jnp.broadcast_to(0.5 * middle, (8, LANES)), 0.0)

    for j in range(parts):
        state = piece(j) - middle
        src_t[j * LANES : (j + 1) * LANES, :] = source_features(state).T.astype(bf16)
        moment = jnp.where(comp < 6, state * state[6:7], jnp.where(comp == 6, state, 0.0))
        high, mid, low = split3(moment)
        rows = jnp.concatenate([high, mid, low, jnp.zeros((8, LANES), f32)], axis=0).astype(bf16)
        packed[j, :, 0:LANES] = rows
        packed[j, :, LANES : 2 * LANES] = rows

    def compact(k, off):
        tile, shift = off // LANES, off % LANES
        rolled = pltpu.roll(tgt_ref[k], shift, 1)
        dense[tile] = jnp.where(lane >= shift, rolled, dense[tile])
        dense[tile + 1] = rolled
        offs[k] = off
        return off + cnt_ref[0, k]

    count = lax.fori_loop(0, n_a, compact, jnp.int32(0))
    tiles = (count + LANES - 1) // LANES

    def tile_step(t, _):
        state = dense[t] - middle
        pair = target_features(state)

        def products_of(c):
            left = src_t[c * SPAN * LANES : (c + 1) * SPAN * LANES, :]
            return [
                jnp.dot(left, pair[:, :LANES], preferred_element_type=f32),
                jnp.dot(left, pair[:, LANES:], preferred_element_type=f32),
            ]

        def weights_of(prod, at):
            tiles_of = [[], [], [], []]
            for g in range(8):
                pulls, twists = [], []
                for h in range(2):
                    row = slice(at + 16 * g + 8 * h, at + 16 * g + 8 * h + 8)
                    radial = prod[0][row]
                    inv = lax.rsqrt(prod[1][row])
                    inv2 = inv * inv
                    pull = inv * inv2
                    pulls.append(pull)
                    twists.append((radial * inv2) * pull)
                for s, both in enumerate((pulls, twists)):
                    full = jnp.concatenate(both, axis=0)
                    high = full.astype(bf16)
                    tiles_of[s].append(high)
                    tiles_of[2 + s].append((full - high.astype(f32)).astype(bf16))
            return [jnp.concatenate(tiles_of[s] + tiles_of[2 + s], axis=0) for s in range(2)]

        acc = [jnp.zeros((32, LANES), f32)] * 2
        groups = parts // SPAN
        ahead = [products_of(c) for c in range(AHEAD)]
        right = None
        for c in range(groups):
            if c + AHEAD < groups:
                ahead.append(products_of(c + AHEAD))
            for u in range(SPAN):
                last, right = right, weights_of(ahead[c], u * LANES)
                if last is not None:
                    acc = [
                        z + jnp.dot(packed[c * SPAN + u - 1], w, preferred_element_type=f32)
                        for z, w in zip(acc, last)
                    ]
        acc = [
            z + jnp.dot(packed[parts - 1], w, preferred_element_type=f32)
            for z, w in zip(acc, right)
        ]
        pull, twist = [z[0:8] + (z[8:16] + z[16:24]) for z in acc]
        force = pull - state * pull[6:7]
        tide = twist - state * twist[6:7]
        jerk = force[3:6] - 3.0 * tide[0:3]
        dense[t] = jnp.concatenate([force[0:3], jerk, jnp.zeros((2, LANES), f32)], axis=0)
        return 0

    lax.fori_loop(0, tiles, tile_step, 0)

    def spread(k, _):
        off = offs[k]
        tile, shift = off // LANES, off % LANES
        both = jnp.where(lane >= shift, dense[tile], dense[tile + 1])
        out_ref[k] = pltpu.roll(both, (LANES - shift) % LANES, 1)
        return 0

    lax.fori_loop(0, n_a, spread, 0)


def return_kernel(n_row, n_col, step_ref, count_ref, part_ref, *refs):
    inputs, outs, rest = refs[:6], refs[6:10], refs[10:]
    local, (load_sem, inbox, send_sem, recv_sem) = rest[:6], rest[6:]
    pos_ref, vel_ref, acc_ref, jerk_ref, time_ref, index_ref = local
    n_a = ROWS * n_col
    loads = [
        pltpu.make_async_copy(a, b, load_sem.at[i]) for i, (a, b) in enumerate(zip(inputs, local))
    ]
    peers = plane_peers(n_col)
    greet(peers)
    for load in loads:
        load.start()
    for load in loads:
        load.wait()
    stars = pos_ref.shape[1]
    pos, vel, acc, jerk = pos_ref[...], vel_ref[...], acc_ref[...], jerk_ref[...]
    span = step_ref[0] - time_ref[...].reshape(1, stars)
    pred_pos, pred_vel = predict(pos, vel, acc, jerk, span)
    pick = one_hot(index_ref[...], count_ref[0, 0], stars)
    pl.semaphore_wait(pltpu.get_barrier_semaphore(), n_a - 1)
    copies = [
        pltpu.make_async_remote_copy(
            src_ref=part_ref.at[slot], dst_ref=inbox.at[back],
            send_sem=send_sem.at[slot], recv_sem=recv_sem.at[back],
            device_id=device, device_id_type=MESH,
        )
        for _, slot, back, device in peers
    ]
    for copy in copies:
        copy.start()
    for copy in copies:
        copy.wait()
    total = part_ref[0]
    for k in range(1, n_a):
        total = total + inbox[k]
    comp = lax.broadcasted_iota(jnp.int32, (8, LANES), 0)
    total = jnp.where(comp < 6, total, 1.0)
    placed = lax.dot_general(
        total, pick, (((1,), (1,)), ((), ())), precision=HIGHEST,
        preferred_element_type=jnp.float32,
    )
    active = placed[6:7] > 0.5
    acc1, jerk1 = placed[0:3], placed[3:6]
    change = acc - acc1
    snap = -6.0 * change - span * (4.0 * jerk + 2.0 * jerk1)
    crack = 12.0 * change + 6.0 * span * (jerk + jerk1)
    out_pos = pred_pos + span * span * (snap / 24.0 + crack / 120.0)
    out_vel = pred_vel + span * (snap / 6.0 + crack / 24.0)
    outs[0][...] = jnp.where(active, out_pos, pos)
    outs[1][...] = jnp.where(active, out_vel, vel)
    outs[2][...] = jnp.where(active, acc1, acc)
    outs[3][...] = jnp.where(active, jerk1, jerk)


def store_kernel(*refs):
    inputs, outs, sem = refs[:4], refs[4:8], refs[8]
    copies = [pltpu.make_async_copy(a, b, sem.at[i]) for i, (a, b) in enumerate(zip(inputs, outs))]
    for copy in copies:
        copy.start()
    for copy in copies:
        copy.wait()


def solution(mesh):
    n_row, n_col = mesh.shape["row"], mesh.shape["col"]
    n_a, n_b = ROWS * n_col, n_row // ROWS
    vmem = pl.BlockSpec(memory_space=pltpu.VMEM)
    smem = pl.BlockSpec(memory_space=pltpu.SMEM)
    hbm = pl.BlockSpec(memory_space=pltpu.HBM)
    f32 = jnp.float32

    def pin(x):
        return pltpu.with_memory_space_constraint(x, pltpu.HBM)

    def per_device(pos, vel, acc, jerk, mass, time, steps, index, count):
        stars = pos.shape[1]
        strength = GRAVITY / (stars * n_row * n_col)
        arrays = (pos, vel, acc, jerk, mass, time, index)
        tgt, src, cnt = pl.pallas_call(
            functools.partial(exchange_kernel, n_row, n_col, strength),
            out_shape=(
                jax.ShapeDtypeStruct((n_a, 8, LANES), f32),
                jax.ShapeDtypeStruct((n_b, 8, stars), f32),
                jax.ShapeDtypeStruct((1, LANES), jnp.int32),
            ),
            in_specs=[smem, smem] + [hbm] * 7,
            out_specs=(vmem, vmem, vmem),
            scratch_shapes=[
                *[pltpu.VMEM(x.shape, x.dtype) for x in arrays],
                pltpu.SemaphoreType.DMA((7,)),
                pltpu.SemaphoreType.DMA((n_a,)),
                pltpu.SemaphoreType.DMA((n_a,)),
                pltpu.SemaphoreType.DMA((n_b,)),
                pltpu.SemaphoreType.DMA((n_b,)),
            ],
            compiler_params=pltpu.CompilerParams(
                collective_id=0, has_side_effects=True, vmem_limit_bytes=GRANT
            ),
            name="exchange",
        )(steps, count, *[pin(x) for x in arrays])
        chunks = n_b * stars // LANES
        part = pl.pallas_call(
            force_kernel,
            out_shape=jax.ShapeDtypeStruct((n_a, 8, LANES), f32),
            in_specs=[smem, vmem, vmem],
            out_specs=vmem,
            scratch_shapes=[
                pltpu.VMEM((n_a + 2, 8, LANES), f32),
                pltpu.VMEM((chunks * LANES, 96), jnp.bfloat16),
                pltpu.VMEM((chunks, 32, 2 * LANES), jnp.bfloat16),
                pltpu.SMEM((n_a,), jnp.int32),
            ],
            compiler_params=pltpu.CompilerParams(vmem_limit_bytes=2 * GRANT),
            name="forces",
        )(cnt, tgt, src)
        arrays = (pos, vel, acc, jerk, time, index)
        news = pl.pallas_call(
            functools.partial(return_kernel, n_row, n_col),
            out_shape=(jax.ShapeDtypeStruct(pos.shape, f32),) * 4,
            in_specs=[smem, smem, vmem] + [hbm] * 6,
            out_specs=(vmem,) * 4,
            scratch_shapes=[
                *[pltpu.VMEM(x.shape, x.dtype) for x in arrays],
                pltpu.SemaphoreType.DMA((6,)),
                pltpu.VMEM((n_a, 8, LANES), f32),
                pltpu.SemaphoreType.DMA((n_a,)),
                pltpu.SemaphoreType.DMA((n_a,)),
            ],
            compiler_params=pltpu.CompilerParams(
                collective_id=1, has_side_effects=True, vmem_limit_bytes=GRANT
            ),
            name="returns",
        )(steps, count, part, *[pin(x) for x in arrays])
        return pl.pallas_call(
            store_kernel,
            out_shape=(jax.ShapeDtypeStruct(pos.shape, f32),) * 4,
            in_specs=[vmem] * 4,
            out_specs=(hbm,) * 4,
            scratch_shapes=[pltpu.SemaphoreType.DMA((4,))],
            compiler_params=pltpu.CompilerParams(vmem_limit_bytes=GRANT),
            name="store",
        )(*news)

    both = ("row", "col")
    state = P(None, both)
    return jax.shard_map(
        per_device,
        mesh=mesh,
        in_specs=(state, state, state, state, P(both), P(both), P(), state, state),
        out_specs=(state, state, state, state),
        check_vma=False,
    )
```

profile of v0, /device:TPU:1, one launch (start us, length us, event | category | flops | bytes accessed | tf_op | source)
XLA Modules:
  0.0 43.6 jit_solution(7589784659060758807)
XLA Ops:
  1.9 16.7 %exchange.1 = (f32[32,8,128]{2,1,0:T(8,128)S(1)}, f32[8,8,384]{2,1,0:T(8,128)S(1)}, s32[1,128]{1,0:T(1,128)S(1)}) custom-call(f32[1]{0:T(128)S(6)} %copy.13.step_ref, s32[1,1]{1,0:T(1,128)S(6)} %copy.14.count_ref, f32[3,384]{1,0:T(4,128)} %refs_0_.3, f32[3,384]{1,0:T(4,128)} %refs_1_.3, f32[3,384]{1,0:T(4,128)} %refs_2_.3, f32[3,384]{1,0:T(4,128)} %refs_3_.3, ...), custom_call_target="tpu_custom_call" | custom-call | tf_op jit(solution)/shard_map/exchange/pallas_call | solution.py:403
  18.6 15.2 %forces.1.part_ref = f32[32,8,128]{2,1,0:T(8,128)S(1)} custom-call(s32[1,128]{1,0:T(1,128)S(1)} %get-tuple-element.11.cnt_ref, f32[32,8,128]{2,1,0:T(8,128)S(1)} %get-tuple-element.12.tgt_ref, f32[8,8,384]{2,1,0:T(8,128)S(1)} %get-tuple-element.13.src_ref), custom_call_target="tpu_custom_call" | custom-call | tf_op jit(solution)/shard_map/forces/pallas_call | solution.py:426
  33.8 9.1 %returns.1 = (f32[3,384]{1,0:T(4,128)S(1)}, f32[3,384]{1,0:T(4,128)S(1)}, f32[3,384]{1,0:T(4,128)S(1)}, f32[3,384]{1,0:T(4,128)S(1)}) custom-call(f32[1]{0:T(128)S(6)} %copy.13.step_ref, s32[1,1]{1,0:T(1,128)S(6)} %copy.14.count_ref, f32[32,8,128]{2,1,0:T(8,128)S(1)} %forces.1.part_ref, f32[3,384]{1,0:T(4,128)} %refs_0_.3, f32[3,384]{1,0:T(4,128)} %refs_1_.3, ...), custom_call_target="tpu_custom_call" | custom-call | tf_op jit(solution)/shard_map/returns/pallas_call | solution.py:441
  42.9 0.6 %store.1 = (f32[3,384]{1,0:T(4,128)}, f32[3,384]{1,0:T(4,128)}, f32[3,384]{1,0:T(4,128)}, f32[3,384]{1,0:T(4,128)}) custom-call(f32[3,384]{1,0:T(4,128)S(1)} %get-tuple-element.14.refs_0_, f32[3,384]{1,0:T(4,128)S(1)} %get-tuple-element.15.refs_1_, f32[3,384]{1,0:T(4,128)S(1)} %get-tuple-element.16.refs_2_, f32[3,384]{1,0:T(4,128)S(1)} %get-tuple-element.17.refs_3_), custom_call_target="tpu_custom_call" | custom-call | tf_op jit(solution)/shard_map/store/pallas_call | solution.py:458
where the time goes:
time: 43.8 us; the launch traced here: 43.6 us
  Pallas kernels  41.6 us (95%)
  between operations  1.94 us (4%)
    pallas_call x1, Pallas kernels, per_device(): pl.pallas_call(functools.partial(exchange_kernel, n_row, n_col, strength)...  16.7 us
    pallas_call x1, Pallas kernels, per_device(): pl.pallas_call(force_kernel, out_shape=jax.ShapeDtypeStruct((n_a, 8, LANE...  15.2 us
    pallas_call x1, Pallas kernels, per_device(): pl.pallas_call(functools.partial(return_kernel, n_row, n_col), out_shape=...  9.07 us

commit v1 on v0

--- a/solution.py
+++ b/solution.py
@@ -106,7 +106,7 @@
     pl.semaphore_wait(pltpu.get_barrier_semaphore(), n_a + n_b - 2)
     far = [
         pltpu.make_async_remote_copy(
-            src_ref=src_ref.at[0], dst_ref=src_ref.at[back],
+            src_ref=src_ref.at[0, 0:7], dst_ref=src_ref.at[back, 0:7],
             send_sem=send_b.at[slot], recv_sem=recv_b.at[back],
             device_id=device, device_id_type=MESH,
         )
@@ -114,7 +114,7 @@
     ]
     wide = [
         pltpu.make_async_remote_copy(
-            src_ref=tgt_ref.at[0], dst_ref=tgt_ref.at[back],
+            src_ref=tgt_ref.at[0, 0:7], dst_ref=tgt_ref.at[back, 0:7],
             send_sem=send_a.at[slot], recv_sem=recv_a.at[back],
             device_id=device, device_id_type=MESH,
         )
@@ -217,7 +217,7 @@
     return jnp.concatenate([radial, square], axis=1).astype(jnp.bfloat16)
 
 
-def force_kernel(cnt_ref, tgt_ref, src_ref, out_ref, dense, src_t, packed, offs):
+def force_kernel(cnt_ref, tgt_ref, src_ref, out_ref, dense, src_t, packed):
     n_a, n_b, stars = tgt_ref.shape[0], src_ref.shape[0], src_ref.shape[2]
     per = stars // LANES
     parts = n_b * per
@@ -244,15 +244,18 @@
         packed[j, :, 0:LANES] = rows
         packed[j, :, LANES : 2 * LANES] = rows
 
-    def compact(k, off):
-        tile, shift = off // LANES, off % LANES
+    count = jnp.int32(0)
+    front = tgt_ref[0]
+    starts = []
+    for k in range(n_a):
+        starts.append(count)
+        tile, shift = lax.div(count, LANES), lax.rem(count, LANES)
         rolled = pltpu.roll(tgt_ref[k], shift, 1)
-        dense[tile] = jnp.where(lane >= shift, rolled, dense[tile])
+        merged = jnp.where(lane >= shift, rolled, front)
+        dense[tile] = merged
         dense[tile + 1] = rolled
-        offs[k] = off
-        return off + cnt_ref[0, k]
-
-    count = lax.fori_loop(0, n_a, compact, jnp.int32(0))
+        count = count + cnt_ref[0, k]
+        front = jnp.where(lax.div(count, LANES) == tile, merged, rolled)
     tiles = (count + LANES - 1) // LANES
 
     def tile_step(t, _):
@@ -312,14 +315,10 @@
 
     lax.fori_loop(0, tiles, tile_step, 0)
 
-    def spread(k, _):
-        off = offs[k]
-        tile, shift = off // LANES, off % LANES
+    for k in range(n_a):
+        tile, shift = lax.div(starts[k], LANES), lax.rem(starts[k], LANES)
         both = jnp.where(lane >= shift, dense[tile], dense[tile + 1])
-        out_ref[k] = pltpu.roll(both, (LANES - shift) % LANES, 1)
-        return 0
-
-    lax.fori_loop(0, n_a, spread, 0)
+        out_ref[k] = pltpu.roll(both, lax.rem(LANES - shift, LANES), 1)
 
 
 def return_kernel(n_row, n_col, step_ref, count_ref, part_ref, *refs):
@@ -344,7 +343,7 @@
     pl.semaphore_wait(pltpu.get_barrier_semaphore(), n_a - 1)
     copies = [
         pltpu.make_async_remote_copy(
-            src_ref=part_ref.at[slot], dst_ref=inbox.at[back],
+            src_ref=part_ref.at[slot, 0:6], dst_ref=inbox.at[back, 0:6],
             send_sem=send_sem.at[slot], recv_sem=recv_sem.at[back],
             device_id=device, device_id_type=MESH,
         )
@@ -432,7 +431,6 @@
                 pltpu.VMEM((n_a + 2, 8, LANES), f32),
                 pltpu.VMEM((chunks * LANES, 96), jnp.bfloat16),
                 pltpu.VMEM((chunks, 32, 2 * LANES), jnp.bfloat16),
-                pltpu.SMEM((n_a,), jnp.int32),
             ],
             compiler_params=pltpu.CompilerParams(vmem_limit_bytes=2 * GRANT),
             name="forces",

time: 43.8 us -> 39 us (0.89)
  the two profiles are of different devices: /device:TPU:1 before, /device:TPU:33 now
where the time goes in v1:
time: 39 us; the launch traced here: 38.3 us
  Pallas kernels  36.4 us (93%)
  between operations  1.94 us (5%)
    pallas_call x1, Pallas kernels, per_device(): pl.pallas_call(functools.partial(exchange_kernel, n_row, n_col, strength)...  14.9 us
    pallas_call x1, Pallas kernels, per_device(): pl.pallas_call(force_kernel, out_shape=jax.ShapeDtypeStruct((n_a, 8, LANE...  12 us
    pallas_call x1, Pallas kernels, per_device(): pl.pallas_call(functools.partial(return_kernel, n_row, n_col), out_shape=...  8.81 us

profile of v1, /device:TPU:33, one launch (start us, length us, event | category | flops | bytes accessed | tf_op | source)
XLA Modules:
  0.0 38.3 jit_solution(4878684308222860643)
XLA Ops:
  1.9 14.9 %exchange.1 = (f32[32,8,128]{2,1,0:T(8,128)S(1)}, f32[8,8,384]{2,1,0:T(8,128)S(1)}, s32[1,128]{1,0:T(1,128)S(1)}) custom-call(f32[1]{0:T(128)S(6)} %copy.13.step_ref, s32[1,1]{1,0:T(1,128)S(6)} %copy.14.count_ref, f32[3,384]{1,0:T(4,128)} %refs_0_.3, f32[3,384]{1,0:T(4,128)} %refs_1_.3, f32[3,384]{1,0:T(4,128)} %refs_2_.3, f32[3,384]{1,0:T(4,128)} %refs_3_.3, ...), custom_call_target="tpu_custom_call" | custom-call | tf_op jit(solution)/shard_map/exchange/pallas_call | solution.py:402
  16.9 12.0 %forces.1.part_ref = f32[32,8,128]{2,1,0:T(8,128)S(1)} custom-call(s32[1,128]{1,0:T(1,128)S(1)} %get-tuple-element.11.cnt_ref, f32[32,8,128]{2,1,0:T(8,128)S(1)} %get-tuple-element.12.tgt_ref, f32[8,8,384]{2,1,0:T(8,128)S(1)} %get-tuple-element.13.src_ref), custom_call_target="tpu_custom_call" | custom-call | tf_op jit(solution)/shard_map/forces/pallas_call | solution.py:425
  28.8 8.8 %returns.1 = (f32[3,384]{1,0:T(4,128)S(1)}, f32[3,384]{1,0:T(4,128)S(1)}, f32[3,384]{1,0:T(4,128)S(1)}, f32[3,384]{1,0:T(4,128)S(1)}) custom-call(f32[1]{0:T(128)S(6)} %copy.13.step_ref, s32[1,1]{1,0:T(1,128)S(6)} %copy.14.count_ref, f32[32,8,128]{2,1,0:T(8,128)S(1)} %forces.1.part_ref, f32[3,384]{1,0:T(4,128)} %refs_0_.3, f32[3,384]{1,0:T(4,128)} %refs_1_.3, ...), custom_call_target="tpu_custom_call" | custom-call | tf_op jit(solution)/shard_map/returns/pallas_call | solution.py:439
  37.7 0.6 %store.1 = (f32[3,384]{1,0:T(4,128)}, f32[3,384]{1,0:T(4,128)}, f32[3,384]{1,0:T(4,128)}, f32[3,384]{1,0:T(4,128)}) custom-call(f32[3,384]{1,0:T(4,128)S(1)} %get-tuple-element.14.refs_0_, f32[3,384]{1,0:T(4,128)S(1)} %get-tuple-element.15.refs_1_, f32[3,384]{1,0:T(4,128)S(1)} %get-tuple-element.16.refs_2_, f32[3,384]{1,0:T(4,128)S(1)} %get-tuple-element.17.refs_3_), custom_call_target="tpu_custom_call" | custom-call | tf_op jit(solution)/shard_map/store/pallas_call | solution.py:456
